TPU v7x, 32 devices: a whole 2x2x4 slice. The times are simulated.
32 devices in a mesh: groups: 2 (over x), space: 16 (over z, y, core).
Axes of the slice: x: 2, y: 2, z: 4, core: 2. Of those that a mesh axis runs over, the one named last changes fastest.
Arguments:
- atom_features: bfloat16 [288, 32, 256], P(('groups', 'space')), parts along dimension 0, may hold values from -6 to 6
- offsets: bfloat16 [288, 3, 32], P(('groups', 'space')), parts along dimension 0, may hold values from 0 to 1
- counts: int32 [288], P(('groups', 'space')), parts along dimension 0, may hold values from 8 to 32, as said below
- radial_weight: bfloat16 [4, 256, 256], replicated, may hold values from -0.375 to 0.375
- charge_weight: bfloat16 [256, 256], replicated, may hold values from -0.375 to 0.375
- wave_filter: float32 [4, 256], replicated, may hold values from -5 to 5
- wavevectors: int32 [3, 1024], replicated, may hold values from -4 to 25, as said below
Outputs:
- updated: bfloat16 [288, 32, 256], P(('groups', 'space')), parts along dimension 0
There are 2 independent parts, one for each index of `groups`. A program takes and returns all parts, laid end to end along the dimension named above; an argument that names none is the same for every part. Nothing has to cross between parts.
Inputs may be any that keep to these rules, and one draw needn't show every extreme that they name: Cell c holds its atoms in its first counts[c] slots; in every draw some cell is full. `wavevectors`: the 1024 columns are distinct index triples from one half of the lattice: no column is zero or the negative of another; the first two indices lie in -4 to 4 and the third in 0 to 25, and where the third is 0 the first is above 0, or the first is 0 and the second above 0.
All inputs are finite; a program needn't handle non-finite values.
Results may differ from a plain program's by a relative error of at most 0.005.
Values may be sent and summed in bfloat16 or wider, within the bound.
A program may use at most 64 MiB of HBM per device.

v0:
```python
import math

import jax
import jax.numpy as jnp
from jax import lax
from jax.sharding import PartitionSpec as P

GRID = 3


CUTOFF = 1.0
block_rows = 512


def with_halo(value, sides, width):
    for axis, dim in sides:
        size, length = (lax.axis_size(axis), value.shape[dim])
        up = [(i, (i + 1) % size) for i in range(size)]
        down = [(j, i) for i, j in up]
        last = lax.slice_in_dim(value, length - width, length, axis=dim)
        leading = lax.slice_in_dim(value, 0, width, axis=dim)
        before = lax.ppermute(last, axis, up)
        after = lax.ppermute(leading, axis, down)
        value = jnp.concatenate([before, value, after], axis=dim)
    return value


def cell_geometry(near_count, cell_slots):
    columns = jnp.arange(near_count * cell_slots, dtype=jnp.int32)
    return (columns // cell_slots, columns % cell_slots)


def pair_radius(own_coords, near_coords, near_cell, near_slot, cell_index, layer_cells):
    own_x = cell_index // GRID
    own_y = cell_index % GRID
    layer_of = near_cell // layer_cells
    within = near_cell % layer_cells
    shift_x = ((within // GRID - own_x + 1) % GRID - 1).astype(jnp.float32)
    shift_y = ((within % GRID - own_y + 1) % GRID - 1).astype(jnp.float32)
    shift_z = (layer_of - 1).astype(jnp.float32)
    own_pos = own_coords.astype(jnp.float32)
    near_pos = near_coords.astype(jnp.float32)
    delta_x = (shift_x + near_pos[0])[None, :] - own_pos[0][:, None]
    delta_y = (shift_y + near_pos[1])[None, :] - own_pos[1][:, None]
    delta_z = (shift_z + near_pos[2])[None, :] - own_pos[2][:, None]
    radius = jnp.sqrt(delta_x * delta_x + delta_y * delta_y + delta_z * delta_z)
    smooth = jnp.where(radius < CUTOFF, 0.5 * (jnp.cos(math.pi * radius / CUTOFF) + 1.0), 0.0)
    slot_ids = jnp.arange(own_pos.shape[1], dtype=jnp.int32)
    itself = (near_cell == layer_cells + cell_index)[None, :] & (
        near_slot[None, :] == slot_ids[:, None]
    )
    return (radius, smooth, itself)


def wave_numbers(wave_rows, layers_total):
    two_pi = 2.0 * math.pi
    wave_float = wave_rows.astype(jnp.float32)
    along_x = two_pi * wave_float[0] / GRID
    along_y = two_pi * wave_float[1] / GRID
    along_z = two_pi * wave_float[2] / layers_total
    return (along_x, along_y, along_z)


def phase_table(positions, wave_rows, layers_total):
    along_x, along_y, along_z = wave_numbers(wave_rows, layers_total)
    return (
        positions[0][:, None] * along_x[None, :]
        + positions[1][:, None] * along_y[None, :]
        + positions[2][:, None] * along_z[None, :]
    )


def structure_terms(positions, charges, wave_rows, layers_total):
    row_count = wave_rows.shape[1]
    feature_width = charges.shape[1]
    pieces = jnp.transpose(wave_rows.reshape(3, row_count // block_rows, block_rows), (1, 0, 2))

    def structure_one_block(wave_block):
        phases = phase_table(positions, wave_block, layers_total)
        cosine = jnp.cos(phases).astype(jnp.bfloat16)
        sine_part = jnp.sin(phases).astype(jnp.bfloat16)
        real_part = lax.dot_general(
            cosine, charges, (((0,), (0,)), ((), ())), preferred_element_type=jnp.float32
        )
        imag_part = lax.dot_general(
            sine_part, charges, (((0,), (0,)), ((), ())), preferred_element_type=jnp.float32
        )
        return jnp.concatenate([real_part, imag_part], axis=1)

    return lax.map(structure_one_block, pieces).reshape(row_count, 2 * feature_width)


def filter_rows(structure, wave_rows, layers_total, wave_filter):
    along_x, along_y, along_z = wave_numbers(wave_rows, layers_total)
    magnitude = jnp.sqrt(along_x * along_x + along_y * along_y + along_z * along_z)
    centres = 3.0 * jnp.arange(wave_filter.shape[0], dtype=jnp.float32)
    offset_k = (magnitude[:, None] - centres[None, :]) / 3.0
    basis_rows = jnp.exp(-(offset_k * offset_k))
    gain_rows = jnp.dot(
        basis_rows, wave_filter, precision=lax.Precision.HIGHEST, preferred_element_type=jnp.float32
    )
    return (structure * jnp.concatenate([gain_rows, gain_rows], axis=1)).astype(jnp.bfloat16)


def add_inverse(running, filtered, wave_rows, positions, layers_total):
    row_count = filtered.shape[0]
    feature_width = filtered.shape[1] // 2
    block_count = row_count // block_rows
    factor_blocks = filtered.reshape(block_count, block_rows, 2 * feature_width)
    wave_blocks = jnp.transpose(wave_rows.reshape(3, block_count, block_rows), (1, 0, 2))

    def add_one_block(summed, block_item):
        factors, wave_block = block_item
        phases = phase_table(positions, wave_block, layers_total)
        cosine = jnp.cos(phases).astype(jnp.bfloat16)
        sine_part = jnp.sin(phases).astype(jnp.bfloat16)
        summed = summed + jnp.dot(
            cosine, factors[:, :feature_width], preferred_element_type=jnp.float32
        )
        summed = summed + jnp.dot(
            sine_part, factors[:, feature_width:], preferred_element_type=jnp.float32
        )
        return (summed, None)

    outcome = lax.scan(add_one_block, running, (factor_blocks, wave_blocks))
    return outcome[0]


def local(atom_features, offsets, counts, radial_weight, charge_weight, wave_filter, wavevectors):
    layer_cells, cell_slots, feature_width = atom_features.shape
    basis_count = radial_weight.shape[0]
    wave_count = wavevectors.shape[1]
    layers_total = lax.axis_size("space")
    layer_index = lax.axis_index("space")
    slot_ids = jnp.arange(cell_slots, dtype=jnp.int32)
    live_mask = (slot_ids[None, :] < counts[:, None]).astype(jnp.float32)
    masked = (atom_features.astype(jnp.float32) * live_mask[:, :, None]).astype(jnp.bfloat16)
    near_features, near_offsets = (
        with_halo(masked, (("space", 0),), layer_cells),
        with_halo(offsets, (("space", 0),), layer_cells),
    )
    near_count = 3 * layer_cells
    near_flat = near_features.reshape(near_count * cell_slots, feature_width)
    near_coords = jnp.transpose(near_offsets, (1, 0, 2)).reshape(3, near_count * cell_slots)
    near_cell, near_slot = cell_geometry(near_count, cell_slots)
    cell_ids = jnp.arange(layer_cells, dtype=jnp.int32)
    values = jnp.stack(
        [
            jnp.dot(
                near_flat, radial_weight[basis_index], preferred_element_type=jnp.float32
            ).astype(jnp.bfloat16)
            for basis_index in range(basis_count)
        ]
    )

    def cell_short(own_coords, cell_index):
        radius, smooth, itself = pair_radius(
            own_coords, near_coords, near_cell, near_slot, cell_index, layer_cells
        )
        running = jnp.zeros((cell_slots, feature_width), jnp.float32)
        for basis_index in range(basis_count):
            centre = (basis_index + 0.5) * CUTOFF / basis_count
            scaled = (radius - centre) * (basis_count / CUTOFF)
            pair_weights = jnp.where(itself, 0.0, jnp.exp(-(scaled * scaled)) * smooth).astype(
                jnp.bfloat16
            )
            running = running + jnp.dot(
                pair_weights, values[basis_index], preferred_element_type=jnp.float32
            )
        return running

    short_sum = jax.vmap(cell_short)(offsets, cell_ids)
    base_x = (cell_ids // GRID).astype(jnp.float32)
    base_y = (cell_ids % GRID).astype(jnp.float32)
    base_z = layer_index.astype(jnp.float32)
    coords = offsets.astype(jnp.float32)
    positions = jnp.stack(
        [
            (base_x[:, None] + coords[:, 0, :]).reshape(-1),
            (base_y[:, None] + coords[:, 1, :]).reshape(-1),
            (base_z + coords[:, 2, :]).reshape(-1),
        ]
    )
    charges = jnp.dot(
        masked.reshape(layer_cells * cell_slots, feature_width),
        charge_weight,
        preferred_element_type=jnp.float32,
    ).astype(jnp.bfloat16)
    empty_sum = jnp.zeros((layer_cells * cell_slots, feature_width), jnp.float32)
    share_rows = wave_count // layers_total
    wave_rows = wavevectors
    own_share = lax.psum_scatter(
        structure_terms(positions, charges, wave_rows, layers_total),
        "space",
        scatter_dimension=0,
        tiled=True,
    )
    own_waves = lax.dynamic_slice_in_dim(wavevectors, layer_index * share_rows, share_rows, 1)
    filtered = filter_rows(own_share, own_waves, layers_total, wave_filter)
    wave_rows = wavevectors
    reciprocal = add_inverse(
        empty_sum,
        lax.all_gather(filtered, "space", axis=0, tiled=True),
        wave_rows,
        positions,
        layers_total,
    )
    short_scaled = short_sum * (1.0 / math.sqrt(cell_slots))
    recip_scaled = reciprocal * (
        1.0 / math.sqrt(layer_cells * layers_total * cell_slots * wave_count)
    )
    combined = (
        atom_features.astype(jnp.float32)
        + short_scaled
        + recip_scaled.reshape(layer_cells, cell_slots, feature_width)
    )
    return (live_mask[:, :, None] * combined).astype(jnp.bfloat16)


def solution(mesh):
    in_specs = (
        P(("groups", "space"), None, None),
        P(("groups", "space"), None, None),
        P(("groups", "space")),
        P(),
        P(),
        P(),
        P(),
    )
    out_specs = P(("groups", "space"), None, None)
    return jax.shard_map(local, mesh=mesh, in_specs=in_specs, out_specs=out_specs, check_vma=False)
```

profile of v0, /device:TPU:0, one launch (start us, length us, event | category | flops | bytes accessed | tf_op | source)
XLA Modules:
  0.0 150.5 jit_solution(8142153261382945371)
XLA Ops:
  8.3 1.0 fusion.102
  9.6 13.8 %while.29 = (s32[]{:T(128)}, f32[2,512,512]{2,1,0:T(8,128)}, f32[9,32]{1,0:T(8,128)}, s32[2,3,512]{2,1,0:T(4,128)}, f32[9,32]{1,0:T(8,128)}, /*index=5*/f32[9,32...) while((s32[]{:T(128)}, f32[2,512,512]{2,1,0:T(8,128)}, ...), condition=%wide.wide.region_1.2_spmd, body=%wide.wide.region_0.1_spmd.sunk | while | flops 153029632 | bytes 7678845 | solution.py:90
  10.3 2.4 %fusion.204 = f32[512,256]{0,1:T(8,128)S(1)} fusion(bf16[288,256]{1,0:T(8,128)(2,1)S(1)} %get-tuple-element.522, f32[512]{0:T(512)S(1)} %bitcast.123, f32[288]{0:T(512)S(1)} %get-tuple-element.523, f32[512]{0:T(512)S(1)} %bitcast.125, f32[288]{0:T(512)S(1)} %get-tuple-element.524, f32[512]{0:T(512)S(1)} %bitcast.121, f32[288]{0:T(512)S(1)} %get-tuple-element.525), kind=kOutput, calls=%fused_computation.5.clone.clone.1 | convolution fusion | flops 76382208 | bytes 681344 | tf_op jit(solution)/shard_map/while/body/eval_jaxpr/dot_general | solution.py:85
  12.7 2.3 %fusion.205 = f32[512,256]{0,1:T(8,128)S(1)} fusion(bf16[288,256]{1,0:T(8,128)(2,1)S(1)} %get-tuple-element.522, f32[512]{0:T(512)S(1)} %bitcast.124, f32[288]{0:T(512)S(1)} %get-tuple-element.523, f32[512]{0:T(512)S(1)} %bitcast.126, f32[288]{0:T(512)S(1)} %get-tuple-element.524, f32[512]{0:T(512)S(1)} %bitcast.122, f32[288]{0:T(512)S(1)} %get-tuple-element.525), kind=kOutput, calls=%fused_computation.4.clone.clone.1 | convolution fusion | flops 76382208 | bytes 681344 | tf_op jit(solution)/shard_map/while/body/eval_jaxpr/dot_general | solution.py:82
  15.4 1.1 constant_dynamic-update-slice_fusion.3
  17.2 2.3 %fusion.204 = f32[512,256]{0,1:T(8,128)S(1)} fusion(bf16[288,256]{1,0:T(8,128)(2,1)S(1)} %get-tuple-element.522, f32[512]{0:T(512)S(1)} %bitcast.123, f32[288]{0:T(512)S(1)} %get-tuple-element.523, f32[512]{0:T(512)S(1)} %bitcast.125, f32[288]{0:T(512)S(1)} %get-tuple-element.524, f32[512]{0:T(512)S(1)} %bitcast.121, f32[288]{0:T(512)S(1)} %get-tuple-element.525), kind=kOutput, calls=%fused_computation.5.clone.clone.1 | convolution fusion | flops 76382208 | bytes 681344 | tf_op jit(solution)/shard_map/while/body/eval_jaxpr/dot_general | solution.py:85
  19.6 2.3 %fusion.205 = f32[512,256]{0,1:T(8,128)S(1)} fusion(bf16[288,256]{1,0:T(8,128)(2,1)S(1)} %get-tuple-element.522, f32[512]{0:T(512)S(1)} %bitcast.124, f32[288]{0:T(512)S(1)} %get-tuple-element.523, f32[512]{0:T(512)S(1)} %bitcast.126, f32[288]{0:T(512)S(1)} %get-tuple-element.524, f32[512]{0:T(512)S(1)} %bitcast.122, f32[288]{0:T(512)S(1)} %get-tuple-element.525), kind=kOutput, calls=%fused_computation.4.clone.clone.1 | convolution fusion | flops 76382208 | bytes 681344 | tf_op jit(solution)/shard_map/while/body/eval_jaxpr/dot_general | solution.py:82
  22.3 1.1 constant_dynamic-update-slice_fusion.3
  23.5 5.5 %collective-permute-start.3 = (bf16[9,32,256]{2,1,0:T(8,128)(2,1)S(1)}, bf16[9,32,256]{2,1,0:T(8,128)(2,1)S(1)}, u32[]{:S(2)}, u32[]{:S(2)}) collective-permute-start(bf16[9,32,256]{2,1,0:T(8,128)(2,1)S(1)} %fusion.102), channel_id=1, source_target_pairs={{1,0},{2,1},{3,2},{4,3},{5,4},{6,5},{7,6},{8,7},{9,8},{10,9},{11,1... | collective-permute-start | bytes 442376 | tf_op jit(solution)/shard_map/ppermute | solution.py:23
  29.0 4.4 %collective-permute-start.1 = (bf16[9,3,32]{2,1,0:T(4,128)(2,1)S(1)}, bf16[9,3,32]{2,1,0:T(4,128)(2,1)S(1)}, u32[]{:S(2)}, u32[]{:S(2)}) collective-permute-start(bf16[9,3,32]{2,1,0:T(4,128)(2,1)S(1)} %copy-done.9), channel_id=1, source_target_pairs={{1,0},{2,1},{3,2},{4,3},{5,4},{6,5},{7,6},{8,7},{9,8},{10,9},{11,1... | collective-permute-start | bytes 5192 | tf_op jit(solution)/shard_map/ppermute | solution.py:23
  34.1 54.0 %reduce-scatter.2.cloned.1.call-done = f32[64,512]{1,0:T(8,128)} async-done(((f32[1024,512]{1,0:T(8,128)}), f32[64,512]{1,0:T(8,128)}) %reduce-scatter.2.cloned.1.call-update) | async-done | bytes 131088 | tf_op jit(solution)/shard_map/reduce_scatter | solution.py:192
  88.1 1.5 %fusion.103 = bf16[64,512]{1,0:T(8,128)(2,1)} fusion(f32[64,512]{1,0:T(8,128)} %reduce-scatter.2.cloned.1.call-done, f32[64,256]{1,0:T(8,128)S(1)} %fusion.145), kind=kLoop, calls=%fused_computation.136 | loop fusion | flops 98304 | bytes 262144 | tf_op jit(solution)/shard_map/convert_element_type | solution.py:102
  90.6 4.6 %fusion.41 = f32[9,32,256]{2,1,0:T(8,128)S(1)} fusion(bf16[864,256]{1,0:T(8,128)(2,1)S(1)} %bitcast.108, f32[9,32]{1,0:T(8,128)S(1)} %get-tuple-element.293, f32[864]{0:T(1024)S(1)} %fusion.141, f32[9,32]{1,0:T(8,128)S(1)} %get-tuple-element.294, f32[9,864]{1,0:T(8,128)S(1)} %get-tuple-element.301, f32[9,32]{1,0:T(8,128)S(1)} %get-tuple-element.292, ...), kind=kOutput, calls=%fused_computation.74 | convolution fusion | flops 246094848 | bytes 1054720 | tf_op jit(solution)/shard_map/vmap()/dot_general | solution.py:167
  95.2 4.6 %convolution_add_fusion.4 = f32[9,32,256]{2,1,0:T(8,128)S(1)} fusion(f32[9,32,256]{2,1,0:T(8,128)S(1)} %fusion.41, bf16[864,256]{1,0:T(8,128)(2,1)S(1)} %bitcast.109, f32[9,32]{1,0:T(8,128)S(1)} %get-tuple-element.293, f32[864]{0:T(1024)S(1)} %fusion.141, f32[9,32]{1,0:T(8,128)S(1)} %get-tuple-element.294, f32[9,864]{1,0:T(8,128)S(1)} %get-tuple-element.301, ...), kind=kOutput, calls=%fused_computation.61 | convolution fusion | flops 246168576 | bytes 1349632 | tf_op jit(solution)/shard_map/vmap()/dot_general | solution.py:167
  99.8 4.8 %convolution_add_fusion.3 = f32[9,32,256]{2,1,0:T(8,128)S(1)} fusion(f32[9,32,256]{2,1,0:T(8,128)S(1)} %convolution_add_fusion.4, bf16[864,256]{1,0:T(8,128)(2,1)S(1)} %bitcast.110, f32[9,32]{1,0:T(8,128)S(1)} %get-tuple-element.293, f32[864]{0:T(1024)S(1)} %fusion.141, f32[9,32]{1,0:T(8,128)S(1)} %get-tuple-element.294, ...), kind=kOutput, calls=%fused_computation.60 | convolution fusion | flops 246168576 | bytes 1349632 | tf_op jit(solution)/shard_map/vmap()/dot_general | solution.py:167
  104.6 22.5 %all-gather.2.cloned.1.call-done = bf16[1024,512]{1,0:T(8,128)(2,1)} async-done(((bf16[64,512]{1,0:T(8,128)(2,1)}), bf16[1024,512]{1,0:T(8,128)(2,1)}) %all-gather.2.cloned.1.call-update) | async-done | bytes 1048592 | tf_op jit(solution)/shard_map/all_gather | solution.py:203
  127.1 11.1 %while.30 = (s32[]{:T(128)}, f32[288,256]{1,0:T(8,128)S(1)}, f32[9,32]{1,0:T(8,128)}, s32[2,3,512]{2,1,0:T(4,128)S(1)}, f32[9,32]{1,0:T(8,128)}, /*index=5*/f32[...) while((s32[]{:T(128)}, f32[288,256]{1,0:T(8,128)S(1)}, ...), condition=%wide.wide.region_4.5_spmd.clone, body=%wide.wide.region_3.4_spmd.clone.sunk | while | flops 152988672 | bytes 2801807 | solution.py:125
  127.2 1.1 dynamic-slice_bitcast_fusion.3
  128.3 2.2 %convolution_add_fusion.9 = f32[288,256]{1,0:T(8,128)S(1)} fusion(f32[288,256]{1,0:T(8,128)S(1)} %get-tuple-element.540, f32[512]{0:T(512)S(1)} %bitcast.117, f32[288]{0:T(512)S(1)} %get-tuple-element.558, f32[512]{0:T(512)S(1)} %bitcast.119, f32[288]{0:T(512)S(1)} %get-tuple-element.559, f32[512]{0:T(512)S(1)} %bitcast.115, ...), kind=kOutput, calls=%fused_computation.24.clone.clone.1 | convolution fusion | flops 76529664 | bytes 864257 | tf_op jit(solution)/shard_map/while/body/eval_jaxpr/dot_general | solution.py:117
  130.5 2.2 %convolution_add_fusion.10 = f32[288,256]{1,0:T(8,128)S(1)} fusion(f32[288,256]{1,0:T(8,128)S(1)} %convolution_add_fusion.9, f32[512]{0:T(512)S(1)} %bitcast.118, f32[288]{0:T(512)S(1)} %get-tuple-element.558, f32[512]{0:T(512)S(1)} %bitcast.120, f32[288]{0:T(512)S(1)} %get-tuple-element.559, f32[512]{0:T(512)S(1)} %bitcast.116, ...), kind=kOutput, calls=%fused_computation.23.clone.clone.1 | convolution fusion | flops 76455936 | bytes 864256 | tf_op jit(solution)/shard_map/while/body/eval_jaxpr/dot_general | solution.py:120
  132.7 1.1 dynamic-slice_bitcast_fusion.3
  133.8 2.2 %convolution_add_fusion.9 = f32[288,256]{1,0:T(8,128)S(1)} fusion(f32[288,256]{1,0:T(8,128)S(1)} %get-tuple-element.540, f32[512]{0:T(512)S(1)} %bitcast.117, f32[288]{0:T(512)S(1)} %get-tuple-element.558, f32[512]{0:T(512)S(1)} %bitcast.119, f32[288]{0:T(512)S(1)} %get-tuple-element.559, f32[512]{0:T(512)S(1)} %bitcast.115, ...), kind=kOutput, calls=%fused_computation.24.clone.clone.1 | convolution fusion | flops 76529664 | bytes 864257 | tf_op jit(solution)/shard_map/while/body/eval_jaxpr/dot_general | solution.py:117
  136.0 2.2 %convolution_add_fusion.10 = f32[288,256]{1,0:T(8,128)S(1)} fusion(f32[288,256]{1,0:T(8,128)S(1)} %convolution_add_fusion.9, f32[512]{0:T(512)S(1)} %bitcast.118, f32[288]{0:T(512)S(1)} %get-tuple-element.558, f32[512]{0:T(512)S(1)} %bitcast.120, f32[288]{0:T(512)S(1)} %get-tuple-element.559, f32[512]{0:T(512)S(1)} %bitcast.116, ...), kind=kOutput, calls=%fused_computation.23.clone.clone.1 | convolution fusion | flops 76455936 | bytes 864256 | tf_op jit(solution)/shard_map/while/body/eval_jaxpr/dot_general | solution.py:120
  138.3 5.3 %fusion.36 = bf16[9,32,256]{2,1,0:T(8,128)(2,1)} fusion(f32[9,32,256]{2,1,0:T(8,128)S(1)} %bitcast.114, f32[9,32,256]{2,1,0:T(8,128)S(1)} %convolution_add_fusion.3, bf16[864,256]{1,0:T(8,128)(2,1)S(1)} %bitcast.111, f32[9,32]{1,0:T(8,128)S(1)} %get-tuple-element.293, f32[864]{0:T(1024)S(1)} %fusion.141, f32[9,32]{1,0:T(8,128)S(1)} %get-tuple-element.294, ...), kind=kOutput, calls=%fused_computation.66 | convolution fusion | flops 246610944 | bytes 1652736 | tf_op jit(solution)/shard_map/vmap()/dot_general | solution.py:167
  (82 shorter events, 5.8 us)
Async XLA Ops:
  6.5 2.8 %copy-start = (bf16[256,256]{1,0:T(8,128)(2,1)S(1)}, bf16[256,256]{1,0:T(8,128)(2,1)}, u32[]{:S(2)}) copy-start(bf16[256,256]{1,0:T(8,128)(2,1)} %param.15) | copy-start | bytes 393220
  6.5 81.6 %reduce-scatter.2.cloned.1.call-start = ((), (), s32[]{:S(2)}) async-start(), calls=%async_computation.1 | async-start | bytes 2228224 | tf_op jit(solution)/shard_map/reduce_scatter | solution.py:192
  8.1 1.5 copy-start.3
  8.1 1.5 copy-start.5
  8.1 1.5 copy-start.7
  23.4 5.6 %copy-start.9 = (bf16[9,3,32]{2,1,0:T(4,128)(2,1)S(1)}, bf16[9,3,32]{2,1,0:T(4,128)(2,1)}, u32[]{:S(2)}) copy-start(bf16[9,3,32]{2,1,0:T(4,128)(2,1)} %param.12) | copy-start | bytes 5188
  23.4 10.1 %copy-start.1 = (s32[2,3,512]{2,1,0:T(4,128)S(1)}, s32[2,3,512]{2,1,0:T(4,128)}, u32[]{:S(2)}) copy-start(s32[2,3,512]{2,1,0:T(4,128)} %get-tuple-element.570) | copy-start | bytes 36868
  23.4 10.4 %copy-start.10 = (f32[4,256]{1,0:T(4,128)S(1)}, f32[4,256]{1,0:T(4,128)}, u32[]{:S(2)}) copy-start(f32[4,256]{1,0:T(4,128)} %param.16) | copy-start | bytes 12292
  23.4 66.4 %copy-start.4 = (f32[9,32]{1,0:T(8,128)S(1)}, f32[9,32]{1,0:T(8,128)}, u32[]{:S(2)}) copy-start(f32[9,32]{1,0:T(8,128)} %get-tuple-element.576) | copy-start | bytes 3460
  23.4 66.5 %copy-start.6 = (f32[9,32]{1,0:T(8,128)S(1)}, f32[9,32]{1,0:T(8,128)}, u32[]{:S(2)}) copy-start(f32[9,32]{1,0:T(8,128)} %get-tuple-element.577) | copy-start | bytes 3460
  23.4 66.5 %copy-start.8 = (f32[9,32]{1,0:T(8,128)S(1)}, f32[9,32]{1,0:T(8,128)}, u32[]{:S(2)}) copy-start(f32[9,32]{1,0:T(8,128)} %get-tuple-element.578) | copy-start | bytes 3460
  23.4 67.2 %copy-start.11 = (bf16[4,256,256]{2,1,0:T(8,128)(2,1)S(1)}, bf16[4,256,256]{2,1,0:T(8,128)(2,1)}, u32[]{:S(2)}) copy-start(bf16[4,256,256]{2,1,0:T(8,128)(2,1)} %param.14) | copy-start | bytes 1572868
  23.4 103.7 %all-gather.2.cloned.1.call-start = ((), (), s32[]{:S(2)}) async-start(), calls=%async_computation.2 | async-start | bytes 1114112 | tf_op jit(solution)/shard_map/all_gather | solution.py:203
  23.5 67.1 %collective-permute-start.3 = (bf16[9,32,256]{2,1,0:T(8,128)(2,1)S(1)}, bf16[9,32,256]{2,1,0:T(8,128)(2,1)S(1)}, u32[]{:S(2)}, u32[]{:S(2)}) collective-permute-start(bf16[9,32,256]{2,1,0:T(8,128)(2,1)S(1)} %fusion.102), channel_id=1, source_target_pairs={{1,0},{2,1},{3,2},{4,3},{5,4},{6,5},{7,6},{8,7},{9,8},{10,9},{11,1... | collective-permute-start | bytes 442376 | tf_op jit(solution)/shard_map/ppermute | solution.py:23
  29.0 61.5 %collective-permute-start.2 = (bf16[9,32,256]{2,1,0:T(8,128)(2,1)S(1)}, bf16[9,32,256]{2,1,0:T(8,128)(2,1)S(1)}, u32[]{:S(2)}, u32[]{:S(2)}) collective-permute-start(bf16[9,32,256]{2,1,0:T(8,128)(2,1)S(1)} %fusion.102), channel_id=1, source_target_pairs={{0,1},{1,2},{2,3},{3,4},{4,5},{5,6},{6,7},{7,8},{8,9},{9,10},{10,1... | collective-permute-start | bytes 442376 | tf_op jit(solution)/shard_map/ppermute | solution.py:22
  29.0 61.0 %collective-permute-start.1 = (bf16[9,3,32]{2,1,0:T(4,128)(2,1)S(1)}, bf16[9,3,32]{2,1,0:T(4,128)(2,1)S(1)}, u32[]{:S(2)}, u32[]{:S(2)}) collective-permute-start(bf16[9,3,32]{2,1,0:T(4,128)(2,1)S(1)} %copy-done.9), channel_id=1, source_target_pairs={{1,0},{2,1},{3,2},{4,3},{5,4},{6,5},{7,6},{8,7},{9,8},{10,9},{11,1... | collective-permute-start | bytes 5192 | tf_op jit(solution)/shard_map/ppermute | solution.py:23
  33.4 56.5 %collective-permute-start = (bf16[9,3,32]{2,1,0:T(4,128)(2,1)S(1)}, bf16[9,3,32]{2,1,0:T(4,128)(2,1)S(1)}, u32[]{:S(2)}, u32[]{:S(2)}) collective-permute-start(bf16[9,3,32]{2,1,0:T(4,128)(2,1)S(1)} %copy-done.9), channel_id=1, source_target_pairs={{0,1},{1,2},{2,3},{3,4},{4,5},{5,6},{6,7},{7,8},{8,9},{9,10},{10,1... | collective-permute-start | bytes 5192 | tf_op jit(solution)/shard_map/ppermute | solution.py:22
  127.1 11.2 %copy-start.2 = (bf16[9,32,256]{2,1,0:T(8,128)(2,1)S(1)}, bf16[9,32,256]{2,1,0:T(8,128)(2,1)}, u32[]{:S(2)}) copy-start(bf16[9,32,256]{2,1,0:T(8,128)(2,1)} %param.11) | copy-start | bytes 442372
Sparse Core Ops, SparseCore 0:
  23.5 64.5 reduce-scatter.1
  90.3 36.7 all-gather.1
where the time goes:
time: 151 us; the launch traced here: 150 us
  waiting for transfers between devices  76.6 us (51%)
  matrix products  38 us (25%)
  between operations  13.7 us (9%)
  starting transfers between devices  10 us (7%)
  other arithmetic  6.27 us (4%)
  local copies, waits for them, and re-layouts  5.82 us (4%)
    reduce_scatter x1, waiting for transfers between devices, local(): lax.psum_scatter(structure_terms(positions, charges, wave_rows, layers_to...  54 us
    all_gather x1, waiting for transfers between devices, local(): lax.all_gather(filtered, 'space', axis=0, tiled=True)  22.5 us
    dot_general x4, matrix products, cell_short(): jnp.dot(pair_weights, values[basis_index], preferred_element_type=jnp.flo...  19.3 us
    ppermute x2, starting transfers between devices, with_halo(): after = lax.ppermute(leading, axis, down)  9.96 us
    dot_general x2, matrix products, structure_one_block(): lax.dot_general(sine_part, charges, (((0,), (0,)), ((), ())), preferred_e...  4.7 us
    dot_general x2, matrix products, structure_one_block(): lax.dot_general(cosine, charges, (((0,), (0,)), ((), ())), preferred_elem...  4.65 us
    dot_general x2, matrix products, add_one_block(): jnp.dot(sine_part, factors[:, feature_width:], preferred_element_type=jnp...  4.45 us
    dot_general x2, matrix products, add_one_block(): jnp.dot(cosine, factors[:, :feature_width], preferred_element_type=jnp.fl...  4.38 us
  transfers between devices with their start and end apart: 6, of which 2 were waited for; matrix products, arithmetic and copies ran while one was open for 11% of the time, Pallas kernels for 0%

commit v1 on v0

v1 whole, which is shorter than its diff:
```python
import functools
import math

import jax
import jax.numpy as jnp
from jax import lax
from jax.experimental import pallas as pl
from jax.experimental.pallas import tpu as pltpu
from jax.sharding import PartitionSpec as P

GRID = 3
MESH = pl.DeviceIdType.MESH
COLORS = 2
F32 = jnp.float32
BF16 = jnp.bfloat16

COS_TURN = (
    0.9999999890590222,
    -19.739204499453972,
    64.93911745989816,
    -85.45013953091984,
    60.167630951184535,
    -25.96759924915613,
    6.528658162048644,
)
SIN_TURN = (
    6.283182793407032,
    -41.34141938561698,
    81.59613875538027,
    -76.57968785100171,
    41.20374363359195,
    -12.268859940903283,
)
COS_HALF_PI = tuple((-1) ** i * (math.pi / 2) ** (2 * i) / math.factorial(2 * i) for i in range(7))


def poly(coefs, x):
    total = coefs[-1] * x + coefs[-2]
    for c in coefs[-3::-1]:
        total = total * x + c
    return total


def layer_kernel(
    dims,
    masked_ref,
    geo_ref,
    gcol_ref,
    wave_ref,
    radial_ref,
    charge_ref,
    filt_ref,
    out_ref,
    halo_x,
    halo_geo,
    near_geo,
    cos_ref,
    sin_ref,
    acc_ref,
    recv_ref,
    full_ref,
    vals_ref,
    pair_ref,
    total_ref,
    halo_send,
    halo_recv,
    send_sem,
    recv_sem,
):
    n, stages, cells, slots, feats, basis, waves, scale_short, scale_recip = dims
    atoms = cells * slots
    rows = 2 * feats // n
    lanes = waves // COLORS
    me = lax.axis_index("space")
    above, below = lax.rem(me + 1, n), lax.rem(me + n - 1, n)

    bits = [(me // 2**j) % 2 for j in range(stages)]
    partners = [me + (1 - 2 * bits[j]) * 2**j for j in range(stages)]
    orders = [list(range(stages)), [0] + list(range(2, stages)) + ([1] if stages > 1 else [])]

    def lo_of(k, s):
        lo = 0
        for t in range(s):
            lo = lo + bits[orders[k][t]] * 2 ** (stages - 1 - t)
        return lo

    def keep_of(k, s):
        return lo_of(k, s) + bits[orders[k][s]] * 2 ** (stages - 1 - s)

    def give_of(k, s):
        return lo_of(k, s) + (1 - bits[orders[k][s]]) * 2 ** (stages - 1 - s)

    barrier = pltpu.get_barrier_semaphore()
    for peer in partners + [above, below]:
        pl.semaphore_signal(barrier, inc=1, device_id={"space": peer}, device_id_type=MESH)
    pl.semaphore_wait(barrier, stages + 2)

    halo = []
    for slot, peer in ((0, above), (1, below)):
        for which, src, dst in ((0, masked_ref, halo_x), (1, geo_ref, halo_geo)):
            copy = pltpu.make_async_remote_copy(
                src_ref=src,
                dst_ref=dst.at[slot],
                send_sem=halo_send.at[slot, which],
                recv_sem=halo_recv.at[slot, which],
                device_id={"space": peer},
                device_id_type=MESH,
            )
            copy.start()
            halo.append(copy)

    def scatter_copy(k, s):
        half = n >> (s + 1)
        return pltpu.make_async_remote_copy(
            src_ref=acc_ref.at[k, pl.ds(give_of(k, s), half)],
            dst_ref=recv_ref.at[k, pl.ds(n - (n >> s), half)],
            send_sem=send_sem.at[k, s],
            recv_sem=recv_sem.at[k, s],
            device_id={"space": partners[orders[k][s]]},
            device_id_type=MESH,
        )

    def gather_copy(k, s):
        half = n >> (s + 1)
        place = full_ref.at[k, pl.ds(keep_of(k, s), half)]
        return pltpu.make_async_remote_copy(
            src_ref=place,
            dst_ref=place,
            send_sem=send_sem.at[k, stages + s],
            recv_sem=recv_sem.at[k, stages + s],
            device_id={"space": partners[orders[k][s]]},
            device_id_type=MESH,
        )

    def scatter_finish(k, s):
        scatter_copy(k, s).wait()
        half = n >> (s + 1)
        keep = keep_of(k, s)
        base = n - (n >> s)
        if s < stages - 1:

            def add_one(i, carry):
                acc_ref[k, keep + i] = (
                    acc_ref[k, keep + i].astype(F32) + recv_ref[k, base + i].astype(F32)
                ).astype(BF16)
                return carry

            lax.fori_loop(0, half, add_one, 0)
            scatter_copy(k, s + 1).start()
        else:
            summed = acc_ref[k, keep].astype(F32) + recv_ref[k, base].astype(F32)
            magnitude = wave_ref[3:4, k * lanes : (k + 1) * lanes]
            weights = filt_ref[keep]
            gain = jnp.zeros((rows, lanes), F32)
            for b in range(basis):
                offset_k = (magnitude - 3.0 * b) * (1.0 / 3.0)
                gain = gain + weights[:, b : b + 1] * jnp.exp(-(offset_k * offset_k))
            full_ref[k, keep] = (summed * gain).astype(BF16)
            gather_copy(k, s).start()

    charges = jnp.dot(masked_ref[...], charge_ref[...], preferred_element_type=F32)
    charges_t = charges.T.astype(BF16)

    for k in range(COLORS):
        span = slice(k * lanes, (k + 1) * lanes)

        def table_rows(i, carry, span=span, k=k):
            at = pl.ds(pl.multiple_of(i * 16, 16), 16)
            turns = (
                gcol_ref[at, 3:4] * wave_ref[0:1, span]
                + gcol_ref[at, 4:5] * wave_ref[1:2, span]
                + gcol_ref[at, 5:6] * wave_ref[2:3, span]
            )
            u = turns - jnp.floor(turns + 0.5)
            sq = u * u
            cos_ref[k, at, :] = poly(COS_TURN, sq).astype(BF16)
            sin_ref[k, at, :] = (u * poly(SIN_TURN, sq)).astype(BF16)
            return carry

        lax.fori_loop(0, atoms // 16, table_rows, 0)
        real = jnp.dot(charges_t, cos_ref[k], preferred_element_type=F32)
        acc_ref[k, 0 : n // 2] = real.reshape(n // 2, rows, lanes).astype(BF16)
        imag = jnp.dot(charges_t, sin_ref[k], preferred_element_type=F32)
        acc_ref[k, n // 2 : n] = imag.reshape(n // 2, rows, lanes).astype(BF16)
        scatter_copy(k, 0).start()

    def near_values(source, layer):
        for b in range(basis):
            vals_ref[b, layer * atoms : (layer + 1) * atoms, :] = jnp.dot(
                source, radial_ref[b], preferred_element_type=F32
            ).astype(BF16)

    def own_values():
        near_values(masked_ref[...], 1)

    def halo_values():
        for copy in halo:
            copy.wait()
        near_values(halo_x[0], 0)
        near_values(halo_x[1], 2)
        near_geo[...] = jnp.concatenate([halo_geo[0], geo_ref[...], halo_geo[1]], axis=1)

    near = 3 * atoms
    mid = basis / 2.0
    group = 16

    def pair_rows(i, carry):
        cell = i // (slots // group)
        start = (i % (slots // group)) * group
        at = pl.ds(pl.multiple_of(i * group, group), group)
        own_x = (cell // GRID).astype(F32)
        own_y = (cell % GRID).astype(F32)
        col = lax.broadcasted_iota(jnp.int32, (1, near), 1)
        shift_x = near_geo[3:4, :] - own_x
        shift_x = jnp.where(shift_x > 1.5, shift_x - GRID, jnp.where(shift_x < -1.5, shift_x + GRID, shift_x))
        shift_y = near_geo[4:5, :] - own_y
        shift_y = jnp.where(shift_y > 1.5, shift_y - GRID, jnp.where(shift_y < -1.5, shift_y + GRID, shift_y))
        shift_z = jnp.where(col < atoms, -1.0, jnp.where(col < 2 * atoms, 0.0, 1.0)).astype(F32)
        dx = (shift_x + near_geo[0:1, :]) - gcol_ref[at, 0:1]
        dy = (shift_y + near_geo[1:2, :]) - gcol_ref[at, 1:2]
        dz = (shift_z + near_geo[2:3, :]) - gcol_ref[at, 2:3]
        sq = dx * dx + dy * dy + dz * dz
        radius = sq * lax.rsqrt(jnp.maximum(sq, 1e-30))
        half_cos = poly(COS_HALF_PI, sq)
        t = jnp.minimum(radius, 1.0) * basis - mid
        row = lax.broadcasted_iota(jnp.int32, (group, near), 0) + start
        itself = (col - (atoms + cell * slots)) == row
        used = (sq < 1.0) & jnp.logical_not(itself)
        core = jnp.where(used, jnp.exp(-(t * t)) * half_cos * half_cos, 0.0)
        grow = jnp.exp(t)
        fall = jnp.exp(-t)
        for b in range(basis):
            d2 = 2 * b + 1 - basis
            weight = core * math.exp(-(d2 * d2) / 4.0)
            if d2 != 0:
                factor = grow if d2 > 0 else fall
                power = factor
                for _ in range(abs(d2) - 1):
                    power = power * factor
                weight = weight * power
            pair_ref[b, at, :] = weight.astype(BF16)
        return carry

    steps = atoms // group

    def pair_span(part, parts):
        lax.fori_loop(part * steps // parts, (part + 1) * steps // parts, pair_rows, 0)

    def short_sum():
        short = jnp.zeros((atoms, feats), F32)
        for b in range(basis):
            short = short + jnp.dot(pair_ref[b], vals_ref[b], preferred_element_type=F32)
        total_ref[...] = short * scale_short

    tasks = [
        own_values,
        halo_values,
        functools.partial(pair_span, 0, 4),
        functools.partial(pair_span, 1, 4),
        functools.partial(pair_span, 2, 4),
        functools.partial(pair_span, 3, 4),
        short_sum,
    ]
    for s in range(stages):
        if tasks:
            tasks.pop(0)()
        for k in range(COLORS):
            scatter_finish(k, s)
    for s in range(stages - 1, -1, -1):
        if tasks:
            tasks.pop(0)()
        for k in range(COLORS):
            gather_copy(k, s).wait()
            if s:
                gather_copy(k, s - 1).start()
    for task in tasks:
        task()

    recip = jnp.zeros((atoms, feats), F32)
    for k in range(COLORS):
        for part, table in ((0, cos_ref), (1, sin_ref)):
            factors = full_ref[k, part * (n // 2) : (part + 1) * (n // 2)].reshape(feats, lanes)
            recip = recip + lax.dot_general(
                table[k], factors, (((1,), (1,)), ((), ())), preferred_element_type=F32
            )
    live = gcol_ref[:, 6:7]
    out_ref[...] = (
        masked_ref[...].astype(F32) + live * (total_ref[...] + recip * scale_recip)
    ).astype(BF16)


def local(atom_features, offsets, counts, radial_weight, charge_weight, wave_filter, wavevectors):
    cells, slots, feats = atom_features.shape
    basis = radial_weight.shape[0]
    waves = wavevectors.shape[1]
    n = lax.axis_size("space")
    layer = lax.axis_index("space")
    stages = n.bit_length() - 1
    assert n == 1 << stages and cells == GRID * GRID
    atoms = cells * slots
    rows = 2 * feats // n
    lanes = waves // COLORS

    slot_ids = jnp.arange(slots, dtype=jnp.int32)
    live = (slot_ids[None, :] < counts[:, None]).astype(F32)
    masked = (atom_features.astype(F32) * live[:, :, None]).astype(BF16).reshape(atoms, feats)
    cell_ids = jnp.arange(cells, dtype=jnp.int32)
    cell_x = jnp.broadcast_to((cell_ids // GRID).astype(F32)[:, None], (cells, slots))
    cell_y = jnp.broadcast_to((cell_ids % GRID).astype(F32)[:, None], (cells, slots))
    off = offsets.astype(F32)
    zero = jnp.zeros_like(cell_x)
    geo = jnp.stack(
        [off[:, 0], off[:, 1], off[:, 2], cell_x, cell_y, zero, zero, zero]
    ).reshape(8, atoms)
    gcol = jnp.stack(
        [
            off[:, 0],
            off[:, 1],
            off[:, 2],
            cell_x + off[:, 0],
            cell_y + off[:, 1],
            layer.astype(F32) + off[:, 2],
            live,
            zero,
        ],
        axis=-1,
    ).reshape(atoms, 8)
    index = wavevectors.astype(F32)
    turns = [index[0] / GRID, index[1] / GRID, index[2] / n]
    along = [2.0 * math.pi * t for t in turns]
    magnitude = jnp.sqrt(along[0] * along[0] + along[1] * along[1] + along[2] * along[2])
    blank = jnp.zeros_like(magnitude)
    wave_rows = jnp.stack(turns + [magnitude] + [blank] * 4)
    filt = jnp.concatenate([wave_filter.T, wave_filter.T]).reshape(n, rows, basis)

    dims = (
        n,
        stages,
        cells,
        slots,
        feats,
        basis,
        waves,
        1.0 / math.sqrt(slots),
        1.0 / math.sqrt(cells * n * slots * waves),
    )
    vmem = pl.BlockSpec(memory_space=pltpu.VMEM)
    out = pl.pallas_call(
        functools.partial(layer_kernel, dims),
        out_shape=jax.ShapeDtypeStruct((atoms, feats), BF16),
        in_specs=[vmem] * 7,
        out_specs=vmem,
        scratch_shapes=[
            pltpu.VMEM((2, atoms, feats), BF16),
            pltpu.VMEM((2, 8, atoms), F32),
            pltpu.VMEM((8, 3 * atoms), F32),
            pltpu.VMEM((COLORS, atoms, lanes), BF16),
            pltpu.VMEM((COLORS, atoms, lanes), BF16),
            pltpu.VMEM((COLORS, n, rows, lanes), BF16),
            pltpu.VMEM((COLORS, n - 1, rows, lanes), BF16),
            pltpu.VMEM((COLORS, n, rows, lanes), BF16),
            pltpu.VMEM((basis, 3 * atoms, feats), BF16),
            pltpu.VMEM((basis, atoms, 3 * atoms), BF16),
            pltpu.VMEM((atoms, feats), F32),
            pltpu.SemaphoreType.DMA((2, 2)),
            pltpu.SemaphoreType.DMA((2, 2)),
            pltpu.SemaphoreType.DMA((COLORS, 2 * stages)),
            pltpu.SemaphoreType.DMA((COLORS, 2 * stages)),
        ],
        compiler_params=pltpu.CompilerParams(collective_id=0, has_side_effects=True),
        name="ewald_layer",
    )(masked, geo, gcol, wave_rows, radial_weight, charge_weight, filt)
    return out.reshape(cells, slots, feats)


def solution(mesh):
    in_specs = (
        P(("groups", "space"), None, None),
        P(("groups", "space"), None, None),
        P(("groups", "space")),
        P(),
        P(),
        P(),
        P(),
    )
    out_specs = P(("groups", "space"), None, None)
    return jax.shard_map(local, mesh=mesh, in_specs=in_specs, out_specs=out_specs, check_vma=False)
```

time: 151 us -> 50.4 us (0.33)
  waiting for transfers between devices: 76.6 us -> 0 us
  Pallas kernels: 0 us -> 41.5 us
  matrix products: 38 us -> 0 us
  between operations: 13.7 us -> 0.06 us
  starting transfers between devices: 10 us -> 0 us
  other arithmetic: 6.27 us -> 0.92 us
  local copies, waits for them, and re-layouts: 5.82 us -> 7.6 us
    reduce_scatter x1 -> x0, waiting for transfers between devices: 54 us -> none  [local(): lax.psum_scatter(structure_terms(positions, charges, wave_rows, layers_to...]
    pallas_call x0 -> x1, Pallas kernels: none -> 41.5 us  [local(): pl.pallas_call(functools.partial(layer_kernel, dims), out_shape=jax.Shape...]
    dot_general x14 -> x0, matrix products: 38 us -> none  [the longest x4 19.3 us: cell_short(): jnp.dot(pair_weights, values[basis_index], preferred_element_type=jnp.flo...]
    all_gather x1 -> x0, waiting for transfers between devices: 22.5 us -> none  [local(): lax.all_gather(filtered, 'space', axis=0, tiled=True)]
    ppermute x4 -> x0, starting transfers between devices: 9.97 us -> none  [the longest x2 9.96 us: with_halo(): after = lax.ppermute(leading, axis, down)]
    convert_element_type x11 -> x7, other arithmetic: 5.54 us -> 0.87 us  [the longest x1 0.77 us: local(): (atom_features.astype(F32) * live[:, :, None]).astype(BF16)]
    unnamed x24 -> x11, local copies, waits for them, and re-layouts: 0.05 us -> 3.45 us
    another operation x0 -> x18, local copies, waits for them, and re-layouts: none -> 2.86 us  [the longest x10 1.15 us: local(): jnp.stack([off[:, 0], off[:, 1], off[:, 2], cell_x, cell_y, zero, zero, z...]
  transfers between devices with their start and end apart: 6 -> 0, of which waited for: 2 -> 0; matrix products, arithmetic and copies ran while one was open for 11% -> 0% of each run, Pallas kernels for 0% -> 0%
where the time goes in v1:
time: 50.4 us; the launch traced here: 50.1 us
  Pallas kernels  41.5 us (82%)
  local copies, waits for them, and re-layouts  7.6 us (15%)
  other arithmetic  0.92 us (2%)
    pallas_call x1, Pallas kernels, local(): pl.pallas_call(functools.partial(layer_kernel, dims), out_shape=jax.Shape...  41.5 us
    unnamed x11, local copies, waits for them, and re-layouts  3.45 us
    another operation x10, local copies, waits for them, and re-layouts, local(): jnp.stack([off[:, 0], off[:, 1], off[:, 2], cell_x, cell_y, zero, zero, z...  1.15 us
    another operation x6, local copies, waits for them, and re-layouts, local(): jnp.stack([off[:, 0], off[:, 1], off[:, 2], cell_x + off[:, 0], cell_y +...  1.06 us

profile of v1, /device:TPU:0, one launch (start us, length us, event | category | flops | bytes accessed | tf_op | source)
XLA Modules:
  0.0 50.1 jit_solution(1800027306957157971)
XLA Ops:
  0.0 0.1 stack_broadcast_in_dim.26
  0.1 0.1 broadcast_in_dim.5
  0.2 0.1 stack_broadcast_in_dim.27
  0.3 0.1 broadcast_in_dim.4
  0.4 0.1 stack_broadcast_in_dim.25
  0.5 0.6 %copy-done.3 = f32[4,256]{1,0:T(4,128)S(1)} copy-done((f32[4,256]{1,0:T(4,128)S(1)}, f32[4,256]{1,0:T(4,128)}, u32[]{:S(2)}) %copy-start.3) | copy-done | bytes 4120
  1.1 0.6 %copy-done.4 = s32[9]{0:T(128)S(1)} copy-done((s32[9]{0:T(128)S(1)}, s32[9]{0:T(128)}, u32[]{:S(2)}) %copy-start.4) | copy-done | bytes 60
  1.8 0.1 fusion
  1.9 0.1 lt.46
  2.0 0.1 lt.45
  2.1 0.5 %copy-done.1 = s32[3,1024]{1,0:T(4,128)S(1)} copy-done((s32[3,1024]{1,0:T(4,128)S(1)}, s32[3,1024]{1,0:T(4,128)}, u32[]{:S(2)}) %copy-start.1) | copy-done | bytes 12312
  2.7 0.6 %stack.45.wave_ref = f32[8,1024]{1,0:T(8,128)} concatenate(f32[1,1024]{1,0:T(1,128)S(1)} %get-tuple-element.11, f32[1,1024]{1,0:T(1,128)S(1)} %get-tuple-element.10, f32[1,1024]{1,0:T(1,128)S(1)} %get-tuple-element.9, f32[1,1024]{1,0:T(1,128)S(1)} %get-tuple-element.8, f32[4,1024]{1,0:T(4,128)S(1)} %stack.44), dimensions={0} | concatenate | bytes 65536 | tf_op jit(solution)/shard_map/stack | solution.py:333
  3.4 0.1 stack.42
  3.5 0.1 stack.37
  3.6 0.1 stack.41
  3.7 0.1 stack.36
  3.8 0.1 stack.40
  3.8 0.1 stack.35
  3.9 0.6 %stack.39.geo_ref = f32[8,288]{1,0:T(8,128)} concatenate(f32[1,288]{1,0:T(1,128)S(1)} %stack.35, f32[1,288]{1,0:T(1,128)S(1)} %stack.36, f32[1,288]{1,0:T(1,128)S(1)} %stack.37, f32[1,288]{1,0:T(1,128)S(1)} %stack_broadcast_in_dim.25, f32[1,288]{1,0:T(1,128)S(1)} %stack_broadcast_in_dim.27, f32[1,288]{1,0:T(1,128)S(1)} %stack_broadcast_in_dim.28, f32[2,288]{1,0:T(2,128)S(1)} %stack.38), dimensions={0} | concatenate | bytes 18432 | tf_op jit(solution)/shard_map/stack | solution.py:312
  4.6 0.8 %copy.21.gcol_ref = f32[288,8]{1,0:T(8,128)} copy(f32[288,8]{0,1:T(8,128)S(1)} %stack.43) | data formatting | bytes 18432 | tf_op jit(solution)/shard_map/stack | solution.py:315
  5.4 0.8 %multiply_convert_fusion = bf16[9,32,256]{2,1,0:T(8,128)(2,1)} fusion(bf16[9,32,256]{2,1,0:T(8,128)(2,1)S(1)} %copy-done, f32[9,32]{1,0:T(8,128)S(1)} %fusion), kind=kLoop, calls=%fused_computation | loop fusion | flops 221184 | bytes 296064 | tf_op jit(solution)/shard_map/convert_element_type | solution.py:306
  6.1 0.8 %copy.20 = f32[512,4]{1,0:T(8,128)} copy(f32[512,4]{0,1:T(4,128)S(1)} %pad_maximum_fusion) | data formatting | bytes 16384 | tf_op jit(solution)/shard_map/concatenate | solution.py:334
  7.0 41.5 %ewald_layer.1 = bf16[288,256]{1,0:T(8,128)(2,1)} custom-call(bf16[288,256]{1,0:T(8,128)(2,1)} %bitcast.7, f32[8,288]{1,0:T(8,128)} %stack.39.geo_ref, f32[288,8]{1,0:T(8,128)} %copy.21.gcol_ref, f32[8,1024]{1,0:T(8,128)} %stack.45.wave_ref, bf16[4,256,256]{2,1,0:T(8,128)(2,1)} %radial_ref.1, bf16[256,256]{1,0:T(8,128)(2,1)} %charge_ref.1, f32[16,32,4]{2,1,0:T(8,128)} %bitcast.6), custom_call_target="tpu_custom_call" | custom-call | tf_op jit(solution)/shard_map/ewald_layer/pallas_call | solution.py:348
  48.5 1.6 %copy.23 = bf16[9,32,256]{2,1,0:T(8,128)(2,1)} copy(bf16[9,32,256]{2,1,0:T(8,128)(2,1)} %bitcast.8) | data formatting | bytes 294912
  (26 shorter events, 0.4 us)
Async XLA Ops:
  0.4 0.7 %copy-start.3 = (f32[4,256]{1,0:T(4,128)S(1)}, f32[4,256]{1,0:T(4,128)}, u32[]{:S(2)}) copy-start(f32[4,256]{1,0:T(4,128)} %param.12) | copy-start | bytes 12292
  1.1 0.7 %copy-start.4 = (s32[9]{0:T(128)S(1)}, s32[9]{0:T(128)}, u32[]{:S(2)}) copy-start(s32[9]{0:T(128)} %param.9) | copy-start | bytes 112
  1.9 0.7 %copy-start.1 = (s32[3,1024]{1,0:T(4,128)S(1)}, s32[3,1024]{1,0:T(4,128)}, u32[]{:S(2)}) copy-start(s32[3,1024]{1,0:T(4,128)} %param.13) | copy-start | bytes 36868
  2.7 0.7 %copy-start.2 = (bf16[9,3,32]{2,1,0:T(4,128)(2,1)S(1)}, bf16[9,3,32]{2,1,0:T(4,128)(2,1)}, u32[]{:S(2)}) copy-start(bf16[9,3,32]{2,1,0:T(4,128)(2,1)} %param.8) | copy-start | bytes 5188
  3.4 1.9 %copy-start = (bf16[9,32,256]{2,1,0:T(8,128)(2,1)S(1)}, bf16[9,32,256]{2,1,0:T(8,128)(2,1)}, u32[]{:S(2)}) copy-start(bf16[9,32,256]{2,1,0:T(8,128)(2,1)} %param.7) | copy-start | bytes 442372

commit v2 on v1

--- a/solution.py
+++ b/solution.py
@@ -10,7 +10,8 @@
 
 GRID = 3
 MESH = pl.DeviceIdType.MESH
-COLORS = 2
+PLANS = (0, 1, 0, 1)
+PARTS = 4
 F32 = jnp.float32
 BF16 = jnp.bfloat16
 
@@ -43,14 +44,25 @@
 
 def layer_kernel(
     dims,
+    counts_ref,
+    x_hbm,
+    off_hbm,
+    wave_hbm,
+    charge_hbm,
+    filter_hbm,
+    radial_hbm,
+    out_ref,
+    x_ref,
+    off_ref,
+    wavei_ref,
+    charge_ref,
+    wfilt_ref,
+    radial_ref,
     masked_ref,
     geo_ref,
     gcol_ref,
     wave_ref,
-    radial_ref,
-    charge_ref,
     filt_ref,
-    out_ref,
     halo_x,
     halo_geo,
     near_geo,
@@ -62,6 +74,7 @@
     vals_ref,
     pair_ref,
     total_ref,
+    load_sem,
     halo_send,
     halo_recv,
     send_sem,
@@ -70,13 +83,15 @@
     n, stages, cells, slots, feats, basis, waves, scale_short, scale_recip = dims
     atoms = cells * slots
     rows = 2 * feats // n
-    lanes = waves // COLORS
+    colors = len(PLANS)
+    lanes = waves // colors
     me = lax.axis_index("space")
     above, below = lax.rem(me + 1, n), lax.rem(me + n - 1, n)
 
     bits = [(me // 2**j) % 2 for j in range(stages)]
     partners = [me + (1 - 2 * bits[j]) * 2**j for j in range(stages)]
-    orders = [list(range(stages)), [0] + list(range(2, stages)) + ([1] if stages > 1 else [])]
+    plans = [list(range(stages)), [0] + list(range(2, stages)) + ([1] if stages > 1 else [])]
+    orders = [plans[p] for p in PLANS]
 
     def lo_of(k, s):
         lo = 0
@@ -93,8 +108,59 @@
     barrier = pltpu.get_barrier_semaphore()
     for peer in partners + [above, below]:
         pl.semaphore_signal(barrier, inc=1, device_id={"space": peer}, device_id_type=MESH)
+
+    loads = [
+        pltpu.make_async_copy(src, dst, load_sem.at[i])
+        for i, (src, dst) in enumerate(
+            (
+                (off_hbm, off_ref),
+                (x_hbm, x_ref),
+                (wave_hbm, wavei_ref),
+                (charge_hbm, charge_ref),
+                (filter_hbm, wfilt_ref),
+                (radial_hbm, radial_ref),
+            )
+        )
+    ]
+    for load in loads:
+        load.start()
+
+    lane = lax.broadcasted_iota(jnp.int32, (1, atoms), 1)
+    cell = lane // slots
+    held = jnp.zeros((1, atoms), jnp.int32)
+    for c in range(cells):
+        held = jnp.where(cell == c, counts_ref[c], held)
+    live_row = jnp.where(lane % slots < held, 1.0, 0.0).astype(F32)
+    cell_x = (cell // GRID).astype(F32)
+    cell_y = (cell % GRID).astype(F32)
+    loads[0].wait()
+    off = jnp.concatenate([off_ref[c].astype(F32) for c in range(cells)], axis=1)
+    geo_ref[...] = jnp.concatenate(
+        [off, cell_x, cell_y, live_row, jnp.zeros((2, atoms), F32)], axis=0
+    )
+    placed = jnp.concatenate(
+        [
+            off,
+            cell_x + off[0:1],
+            cell_y + off[1:2],
+            me.astype(F32) + off[2:3],
+            live_row,
+            jnp.zeros((1, atoms), F32),
+        ],
+        axis=0,
+    )
+    gcol_ref[...] = placed.T
+    loads[1].wait()
+    masked_ref[...] = (
+        x_ref[...].reshape(atoms, feats).astype(F32) * gcol_ref[:, 6:7]
+    ).astype(BF16)
+    loads[2].wait()
+    wave = wavei_ref[...].astype(F32)
+    tx, ty, tz = wave[0:1] * (1.0 / GRID), wave[1:2] * (1.0 / GRID), wave[2:3] * (1.0 / n)
+    length = (2.0 * math.pi) * jnp.sqrt(tx * tx + ty * ty + tz * tz)
+    wave_ref[...] = jnp.concatenate([tx, ty, tz, length, jnp.zeros((4, waves), F32)], axis=0)
+
     pl.semaphore_wait(barrier, stages + 2)
-
     halo = []
     for slot, peer in ((0, above), (1, below)):
         for which, src, dst in ((0, masked_ref, halo_x), (1, geo_ref, halo_geo)):
@@ -106,7 +172,6 @@
                 device_id={"space": peer},
                 device_id_type=MESH,
             )
-            copy.start()
             halo.append(copy)
 
     def scatter_copy(k, s):
@@ -158,14 +223,33 @@
             full_ref[k, keep] = (summed * gain).astype(BF16)
             gather_copy(k, s).start()
 
+    def inverse(k):
+        recip = jnp.zeros((atoms, feats), F32)
+        for part, table in ((0, cos_ref), (1, sin_ref)):
+            factors = full_ref[k, part * (n // 2) : (part + 1) * (n // 2)].reshape(feats, lanes)
+            recip = recip + lax.dot_general(
+                table[k], factors, (((1,), (1,)), ((), ())), preferred_element_type=F32
+            )
+        total_ref[...] = total_ref[...] + recip * scale_recip
+
+    def exchange(k, step):
+        if step < stages:
+            scatter_finish(k, step)
+        else:
+            s = 2 * stages - 1 - step
+            gather_copy(k, s).wait()
+            if s:
+                gather_copy(k, s - 1).start()
+
+    loads[3].wait()
     charges = jnp.dot(masked_ref[...], charge_ref[...], preferred_element_type=F32)
     charges_t = charges.T.astype(BF16)
 
-    for k in range(COLORS):
+    def tables(k):
         span = slice(k * lanes, (k + 1) * lanes)
 
-        def table_rows(i, carry, span=span, k=k):
-            at = pl.ds(pl.multiple_of(i * 16, 16), 16)
+        def table_rows(i, carry):
+            at = pl.ds(pl.multiple_of(i * 32, 32), 32)
             turns = (
                 gcol_ref[at, 3:4] * wave_ref[0:1, span]
                 + gcol_ref[at, 4:5] * wave_ref[1:2, span]
@@ -177,7 +261,7 @@
             sin_ref[k, at, :] = (u * poly(SIN_TURN, sq)).astype(BF16)
             return carry
 
-        lax.fori_loop(0, atoms // 16, table_rows, 0)
+        lax.fori_loop(0, atoms // 32, table_rows, 0)
         real = jnp.dot(charges_t, cos_ref[k], preferred_element_type=F32)
         acc_ref[k, 0 : n // 2] = real.reshape(n // 2, rows, lanes).astype(BF16)
         imag = jnp.dot(charges_t, sin_ref[k], preferred_element_type=F32)
@@ -191,6 +275,14 @@
             ).astype(BF16)
 
     def own_values():
+        loads[4].wait()
+        loads[5].wait()
+        wide = filt_ref.shape[-1]
+        weights = jnp.concatenate(
+            [wfilt_ref[...], jnp.zeros((wide - basis, feats), F32)], axis=0
+        ).T.reshape(n // 2, rows, wide)
+        filt_ref[0 : n // 2] = weights
+        filt_ref[n // 2 : n] = weights
         near_values(masked_ref[...], 1)
 
     def halo_values():
@@ -252,41 +344,34 @@
             short = short + jnp.dot(pair_ref[b], vals_ref[b], preferred_element_type=F32)
         total_ref[...] = short * scale_short
 
-    tasks = [
-        own_values,
-        halo_values,
-        functools.partial(pair_span, 0, 4),
-        functools.partial(pair_span, 1, 4),
-        functools.partial(pair_span, 2, 4),
-        functools.partial(pair_span, 3, 4),
-        short_sum,
-    ]
-    for s in range(stages):
+    for k in range(colors):
+        tables(k)
+        if k == 0:
+            for copy in halo:
+                copy.start()
+        for j in range(k):
+            exchange(j, k - 1 - j)
+
+    tasks = [own_values, halo_values]
+    tasks += [functools.partial(pair_span, part, PARTS) for part in range(PARTS)] + [short_sum]
+    done = [colors - 1 - j for j in range(colors)]
+    while any(step < 2 * stages for step in done):
         if tasks:
             tasks.pop(0)()
-        for k in range(COLORS):
-            scatter_finish(k, s)
-    for s in range(stages - 1, -1, -1):
-        if tasks:
-            tasks.pop(0)()
-        for k in range(COLORS):
-            gather_copy(k, s).wait()
-            if s:
-                gather_copy(k, s - 1).start()
-    for task in tasks:
-        task()
-
-    recip = jnp.zeros((atoms, feats), F32)
-    for k in range(COLORS):
-        for part, table in ((0, cos_ref), (1, sin_ref)):
-            factors = full_ref[k, part * (n // 2) : (part + 1) * (n // 2)].reshape(feats, lanes)
-            recip = recip + lax.dot_general(
-                table[k], factors, (((1,), (1,)), ((), ())), preferred_element_type=F32
-            )
-    live = gcol_ref[:, 6:7]
+        for k in range(colors):
+            if done[k] < 2 * stages:
+                exchange(k, done[k])
+                done[k] += 1
+                if done[k] == 2 * stages:
+                    while tasks:
+                        tasks.pop(0)()
+                    inverse(k)
+
     out_ref[...] = (
-        masked_ref[...].astype(F32) + live * (total_ref[...] + recip * scale_recip)
-    ).astype(BF16)
+        (masked_ref[...].astype(F32) + gcol_ref[:, 6:7] * total_ref[...])
+        .astype(BF16)
+        .reshape(cells, slots, feats)
+    )
 
 
 def local(atom_features, offsets, counts, radial_weight, charge_weight, wave_filter, wavevectors):
@@ -294,45 +379,12 @@
     basis = radial_weight.shape[0]
     waves = wavevectors.shape[1]
     n = lax.axis_size("space")
-    layer = lax.axis_index("space")
     stages = n.bit_length() - 1
     assert n == 1 << stages and cells == GRID * GRID
     atoms = cells * slots
     rows = 2 * feats // n
-    lanes = waves // COLORS
-
-    slot_ids = jnp.arange(slots, dtype=jnp.int32)
-    live = (slot_ids[None, :] < counts[:, None]).astype(F32)
-    masked = (atom_features.astype(F32) * live[:, :, None]).astype(BF16).reshape(atoms, feats)
-    cell_ids = jnp.arange(cells, dtype=jnp.int32)
-    cell_x = jnp.broadcast_to((cell_ids // GRID).astype(F32)[:, None], (cells, slots))
-    cell_y = jnp.broadcast_to((cell_ids % GRID).astype(F32)[:, None], (cells, slots))
-    off = offsets.astype(F32)
-    zero = jnp.zeros_like(cell_x)
-    geo = jnp.stack(
-        [off[:, 0], off[:, 1], off[:, 2], cell_x, cell_y, zero, zero, zero]
-    ).reshape(8, atoms)
-    gcol = jnp.stack(
-        [
-            off[:, 0],
-            off[:, 1],
-            off[:, 2],
-            cell_x + off[:, 0],
-            cell_y + off[:, 1],
-            layer.astype(F32) + off[:, 2],
-            live,
-            zero,
-        ],
-        axis=-1,
-    ).reshape(atoms, 8)
-    index = wavevectors.astype(F32)
-    turns = [index[0] / GRID, index[1] / GRID, index[2] / n]
-    along = [2.0 * math.pi * t for t in turns]
-    magnitude = jnp.sqrt(along[0] * along[0] + along[1] * along[1] + along[2] * along[2])
-    blank = jnp.zeros_like(magnitude)
-    wave_rows = jnp.stack(turns + [magnitude] + [blank] * 4)
-    filt = jnp.concatenate([wave_filter.T, wave_filter.T]).reshape(n, rows, basis)
-
+    colors = len(PLANS)
+    lanes = waves // colors
     dims = (
         n,
         stages,
@@ -344,33 +396,45 @@
         1.0 / math.sqrt(slots),
         1.0 / math.sqrt(cells * n * slots * waves),
     )
-    vmem = pl.BlockSpec(memory_space=pltpu.VMEM)
-    out = pl.pallas_call(
+    anyspace = pl.BlockSpec(memory_space=pl.ANY)
+    args = (counts, atom_features, offsets, wavevectors, charge_weight, wave_filter, radial_weight)
+    return pl.pallas_call(
         functools.partial(layer_kernel, dims),
-        out_shape=jax.ShapeDtypeStruct((atoms, feats), BF16),
-        in_specs=[vmem] * 7,
-        out_specs=vmem,
+        out_shape=jax.ShapeDtypeStruct((cells, slots, feats), BF16),
+        in_specs=[pl.BlockSpec(memory_space=pltpu.SMEM)] + [anyspace] * 6,
+        out_specs=pl.BlockSpec(memory_space=pltpu.VMEM),
         scratch_shapes=[
+            pltpu.VMEM(atom_features.shape, BF16),
+            pltpu.VMEM(offsets.shape, BF16),
+            pltpu.VMEM(wavevectors.shape, jnp.int32),
+            pltpu.VMEM(charge_weight.shape, BF16),
+            pltpu.VMEM(wave_filter.shape, F32),
+            pltpu.VMEM(radial_weight.shape, BF16),
+            pltpu.VMEM((atoms, feats), BF16),
+            pltpu.VMEM((8, atoms), F32),
+            pltpu.VMEM((atoms, 8), F32),
+            pltpu.VMEM((8, waves), F32),
+            pltpu.VMEM((n, rows, basis + -basis % 8), F32),
             pltpu.VMEM((2, atoms, feats), BF16),
             pltpu.VMEM((2, 8, atoms), F32),
             pltpu.VMEM((8, 3 * atoms), F32),
-            pltpu.VMEM((COLORS, atoms, lanes), BF16),
-            pltpu.VMEM((COLORS, atoms, lanes), BF16),
-            pltpu.VMEM((COLORS, n, rows, lanes), BF16),
-            pltpu.VMEM((COLORS, n - 1, rows, lanes), BF16),
-            pltpu.VMEM((COLORS, n, rows, lanes), BF16),
+            pltpu.VMEM((colors, atoms, lanes), BF16),
+            pltpu.VMEM((colors, atoms, lanes), BF16),
+            pltpu.VMEM((colors, n, rows, lanes), BF16),
+            pltpu.VMEM((colors, n - 1, rows, lanes), BF16),
+            pltpu.VMEM((colors, n, rows, lanes), BF16),
             pltpu.VMEM((basis, 3 * atoms, feats), BF16),
             pltpu.VMEM((basis, atoms, 3 * atoms), BF16),
             pltpu.VMEM((atoms, feats), F32),
+            pltpu.SemaphoreType.DMA((6,)),
             pltpu.SemaphoreType.DMA((2, 2)),
             pltpu.SemaphoreType.DMA((2, 2)),
-            pltpu.SemaphoreType.DMA((COLORS, 2 * stages)),
-            pltpu.SemaphoreType.DMA((COLORS, 2 * stages)),
+            pltpu.SemaphoreType.DMA((colors, 2 * stages)),
+            pltpu.SemaphoreType.DMA((colors, 2 * stages)),
         ],
         compiler_params=pltpu.CompilerParams(collective_id=0, has_side_effects=True),
         name="ewald_layer",
-    )(masked, geo, gcol, wave_rows, radial_weight, charge_weight, filt)
-    return out.reshape(cells, slots, feats)
+    )(*args)
 
 
 def solution(mesh):

time: 50.4 us -> 46.6 us (0.925)
  local copies, waits for them, and re-layouts: 7.6 us -> 1.58 us
  Pallas kernels: 41.5 us -> 44.8 us
  other arithmetic: 0.92 us -> 0 us
    pallas_call x1, Pallas kernels: 41.5 us -> 44.8 us  [local(): pl.pallas_call(functools.partial(layer_kernel, dims), out_shape=jax.Shape...]
    another operation x18 -> x0, local copies, waits for them, and re-layouts: 2.86 us -> none  [the longest x10 1.15 us: local(): jnp.stack([off[:, 0], off[:, 1], off[:, 2], cell_x, cell_y, zero, zero, z...]
    unnamed x11 -> x1, local copies, waits for them, and re-layouts: 3.45 us -> 1.58 us
    convert_element_type x7 -> x0, other arithmetic: 0.87 us -> none  [the longest x1 0.77 us: local(): (atom_features.astype(F32) * live[:, :, None]).astype(BF16)]
    concatenate x1 -> x0, local copies, waits for them, and re-layouts: 0.85 us -> none  [local(): jnp.concatenate([wave_filter.T, wave_filter.T]).reshape(n, rows, basis)]
where the time goes in v2:
time: 46.6 us; the launch traced here: 46.4 us
  Pallas kernels  44.8 us (96%)
  local copies, waits for them, and re-layouts  1.58 us (3%)
    pallas_call x1, Pallas kernels, local(): pl.pallas_call(functools.partial(layer_kernel, dims), out_shape=jax.Shape...  44.8 us
    unnamed x1, local copies, waits for them, and re-layouts  1.58 us

profile of v2, /device:TPU:0, one launch (start us, length us, event | category | flops | bytes accessed | tf_op | source)
XLA Modules:
  0.0 46.4 jit_solution(1604845160693617242)
XLA Ops:
  0.0 44.8 %ewald_layer.1 = bf16[9,32,256]{2,1,0:T(8,128)(2,1)} custom-call(s32[9]{0:T(128)} %counts_ref.1, bf16[9,32,256]{2,1,0:T(8,128)(2,1)} %x_hbm.1, bf16[9,3,32]{2,1,0:T(4,128)(2,1)} %off_hbm.1, s32[3,1024]{1,0:T(4,128)} %wave_hbm.1, bf16[256,256]{1,0:T(8,128)(2,1)} %charge_hbm.1, f32[4,256]{1,0:T(4,128)} %filter_hbm.1, bf16[4,256,256]{2,1,0:T(8,128)(2,1)} %radial_hbm.1), custom_call_target="tpu_custom_call" | custom-call | tf_op jit(solution)/shard_map/ewald_layer/pallas_call | solution.py:401
  44.8 1.6 %copy.9 = bf16[9,32,256]{2,1,0:T(8,128)(2,1)} copy(bf16[9,32,256]{2,1,0:T(8,128)(2,1)} %ewald_layer.1) | data formatting | bytes 294912

commit v3 on v2

--- a/solution.py
+++ b/solution.py
@@ -10,7 +10,7 @@
 
 GRID = 3
 MESH = pl.DeviceIdType.MESH
-PLANS = (0, 1, 0, 1)
+PLANS = (1, 0)
 PARTS = 4
 F32 = jnp.float32
 BF16 = jnp.bfloat16
@@ -80,7 +80,7 @@
     send_sem,
     recv_sem,
 ):
-    n, stages, cells, slots, feats, basis, waves, scale_short, scale_recip = dims
+    n, widths, cells, slots, feats, basis, waves, scale_short, scale_recip = dims
     atoms = cells * slots
     rows = 2 * feats // n
     colors = len(PLANS)
@@ -88,25 +88,31 @@
     me = lax.axis_index("space")
     above, below = lax.rem(me + 1, n), lax.rem(me + n - 1, n)
 
-    bits = [(me // 2**j) % 2 for j in range(stages)]
-    partners = [me + (1 - 2 * bits[j]) * 2**j for j in range(stages)]
+    stages = len(widths)
+    bases = [math.prod(widths[:j]) for j in range(stages)]
+    digits = [(me // bases[j]) % widths[j] for j in range(stages)]
+    partners = [
+        [me + ((digits[j] + d) % widths[j] - digits[j]) * bases[j] for d in range(1, widths[j])]
+        for j in range(stages)
+    ]
     plans = [list(range(stages)), [0] + list(range(2, stages)) + ([1] if stages > 1 else [])]
     orders = [plans[p] for p in PLANS]
+
+    def size_of(k, s):
+        size = n
+        for t in range(s):
+            size = size // widths[orders[k][t]]
+        return size
 
     def lo_of(k, s):
         lo = 0
         for t in range(s):
-            lo = lo + bits[orders[k][t]] * 2 ** (stages - 1 - t)
+            lo = lo + digits[orders[k][t]] * size_of(k, t + 1)
         return lo
 
-    def keep_of(k, s):
-        return lo_of(k, s) + bits[orders[k][s]] * 2 ** (stages - 1 - s)
-
-    def give_of(k, s):
-        return lo_of(k, s) + (1 - bits[orders[k][s]]) * 2 ** (stages - 1 - s)
-
     barrier = pltpu.get_barrier_semaphore()
-    for peer in partners + [above, below]:
+    peers = [peer for group_of in partners for peer in group_of] + [above, below]
+    for peer in peers:
         pl.semaphore_signal(barrier, inc=1, device_id={"space": peer}, device_id_type=MESH)
 
     loads = [
@@ -160,7 +166,7 @@
     length = (2.0 * math.pi) * jnp.sqrt(tx * tx + ty * ty + tz * tz)
     wave_ref[...] = jnp.concatenate([tx, ty, tz, length, jnp.zeros((4, waves), F32)], axis=0)
 
-    pl.semaphore_wait(barrier, stages + 2)
+    pl.semaphore_wait(barrier, len(peers))
     halo = []
     for slot, peer in ((0, above), (1, below)):
         for which, src, dst in ((0, masked_ref, halo_x), (1, geo_ref, halo_geo)):
@@ -174,46 +180,71 @@
             )
             halo.append(copy)
 
-    def scatter_copy(k, s):
-        half = n >> (s + 1)
-        return pltpu.make_async_remote_copy(
-            src_ref=acc_ref.at[k, pl.ds(give_of(k, s), half)],
-            dst_ref=recv_ref.at[k, pl.ds(n - (n >> s), half)],
-            send_sem=send_sem.at[k, s],
-            recv_sem=recv_sem.at[k, s],
-            device_id={"space": partners[orders[k][s]]},
-            device_id_type=MESH,
-        )
-
-    def gather_copy(k, s):
-        half = n >> (s + 1)
-        place = full_ref.at[k, pl.ds(keep_of(k, s), half)]
-        return pltpu.make_async_remote_copy(
-            src_ref=place,
-            dst_ref=place,
-            send_sem=send_sem.at[k, stages + s],
-            recv_sem=recv_sem.at[k, stages + s],
-            device_id={"space": partners[orders[k][s]]},
-            device_id_type=MESH,
-        )
+    def scatter_copies(k, s):
+        digit = orders[k][s]
+        part = size_of(k, s + 1)
+        base = n - size_of(k, s)
+        return [
+            pltpu.make_async_remote_copy(
+                src_ref=acc_ref.at[
+                    k, pl.ds(lo_of(k, s) + (digits[digit] + d) % widths[digit] * part, part)
+                ],
+                dst_ref=recv_ref.at[k, pl.ds(base + (d - 1) * part, part)],
+                send_sem=send_sem.at[k, s, d - 1],
+                recv_sem=recv_sem.at[k, s, d - 1],
+                device_id={"space": partners[digit][d - 1]},
+                device_id_type=MESH,
+            )
+            for d in range(1, widths[digit])
+        ]
+
+    def gather_copies(k, s):
+        digit = orders[k][s]
+        part = size_of(k, s + 1)
+        place = full_ref.at[k, pl.ds(lo_of(k, s + 1), part)]
+        return [
+            pltpu.make_async_remote_copy(
+                src_ref=place,
+                dst_ref=place,
+                send_sem=send_sem.at[k, stages + s, d - 1],
+                recv_sem=recv_sem.at[k, stages + s, d - 1],
+                device_id={"space": partners[digit][d - 1]},
+                device_id_type=MESH,
+            )
+            for d in range(1, widths[digit])
+        ]
+
+    def start_all(copies):
+        for copy in copies:
+            copy.start()
+
+    def wait_all(copies):
+        for copy in copies:
+            copy.wait()
 
     def scatter_finish(k, s):
-        scatter_copy(k, s).wait()
-        half = n >> (s + 1)
-        keep = keep_of(k, s)
-        base = n - (n >> s)
+        wait_all(scatter_copies(k, s))
+        part = size_of(k, s + 1)
+        keep = lo_of(k, s + 1)
+        base = n - size_of(k, s)
+        others = widths[orders[k][s]] - 1
+
+        def sum_of(i):
+            total = acc_ref[k, keep + i].astype(F32)
+            for d in range(others):
+                total = total + recv_ref[k, base + d * part + i].astype(F32)
+            return total
+
         if s < stages - 1:
 
             def add_one(i, carry):
-                acc_ref[k, keep + i] = (
-                    acc_ref[k, keep + i].astype(F32) + recv_ref[k, base + i].astype(F32)
-                ).astype(BF16)
+                acc_ref[k, keep + i] = sum_of(i).astype(BF16)
                 return carry
 
-            lax.fori_loop(0, half, add_one, 0)
-            scatter_copy(k, s + 1).start()
+            lax.fori_loop(0, part, add_one, 0)
+            start_all(scatter_copies(k, s + 1))
         else:
-            summed = acc_ref[k, keep].astype(F32) + recv_ref[k, base].astype(F32)
+            summed = sum_of(0)
             magnitude = wave_ref[3:4, k * lanes : (k + 1) * lanes]
             weights = filt_ref[keep]
             gain = jnp.zeros((rows, lanes), F32)
@@ -221,7 +252,7 @@
                 offset_k = (magnitude - 3.0 * b) * (1.0 / 3.0)
                 gain = gain + weights[:, b : b + 1] * jnp.exp(-(offset_k * offset_k))
             full_ref[k, keep] = (summed * gain).astype(BF16)
-            gather_copy(k, s).start()
+            start_all(gather_copies(k, s))
 
     def inverse(k):
         recip = jnp.zeros((atoms, feats), F32)
@@ -237,15 +268,15 @@
             scatter_finish(k, step)
         else:
             s = 2 * stages - 1 - step
-            gather_copy(k, s).wait()
+            wait_all(gather_copies(k, s))
             if s:
-                gather_copy(k, s - 1).start()
+                start_all(gather_copies(k, s - 1))
 
     loads[3].wait()
     charges = jnp.dot(masked_ref[...], charge_ref[...], preferred_element_type=F32)
     charges_t = charges.T.astype(BF16)
 
-    def tables(k):
+    def tables(k, between):
         span = slice(k * lanes, (k + 1) * lanes)
 
         def table_rows(i, carry):
@@ -262,11 +293,12 @@
             return carry
 
         lax.fori_loop(0, atoms // 32, table_rows, 0)
+        between()
         real = jnp.dot(charges_t, cos_ref[k], preferred_element_type=F32)
         acc_ref[k, 0 : n // 2] = real.reshape(n // 2, rows, lanes).astype(BF16)
         imag = jnp.dot(charges_t, sin_ref[k], preferred_element_type=F32)
         acc_ref[k, n // 2 : n] = imag.reshape(n // 2, rows, lanes).astype(BF16)
-        scatter_copy(k, 0).start()
+        start_all(scatter_copies(k, 0))
 
     def near_values(source, layer):
         for b in range(basis):
@@ -285,12 +317,14 @@
         filt_ref[n // 2 : n] = weights
         near_values(masked_ref[...], 1)
 
+    def halo_places():
+        wait_all(halo[1::2])
+        near_geo[...] = jnp.concatenate([halo_geo[0], geo_ref[...], halo_geo[1]], axis=1)
+
     def halo_values():
-        for copy in halo:
-            copy.wait()
+        wait_all(halo[0::2])
         near_values(halo_x[0], 0)
         near_values(halo_x[1], 2)
-        near_geo[...] = jnp.concatenate([halo_geo[0], geo_ref[...], halo_geo[1]], axis=1)
 
     near = 3 * atoms
     mid = basis / 2.0
@@ -344,28 +378,25 @@
             short = short + jnp.dot(pair_ref[b], vals_ref[b], preferred_element_type=F32)
         total_ref[...] = short * scale_short
 
+    start_all(halo[1::2])
     for k in range(colors):
-        tables(k)
-        if k == 0:
-            for copy in halo:
-                copy.start()
-        for j in range(k):
-            exchange(j, k - 1 - j)
-
-    tasks = [own_values, halo_values]
-    tasks += [functools.partial(pair_span, part, PARTS) for part in range(PARTS)] + [short_sum]
-    done = [colors - 1 - j for j in range(colors)]
-    while any(step < 2 * stages for step in done):
-        if tasks:
-            tasks.pop(0)()
-        for k in range(colors):
-            if done[k] < 2 * stages:
-                exchange(k, done[k])
-                done[k] += 1
-                if done[k] == 2 * stages:
-                    while tasks:
-                        tasks.pop(0)()
-                    inverse(k)
+        tables(k, functools.partial(exchange, k - 1, 0) if k else lambda: None)
+    exchange(colors - 1, 0)
+
+    spans = [functools.partial(pair_span, part, PARTS) for part in range(PARTS)]
+    tasks = {1: [own_values, halo_places] + spans[:2], 2: spans[2:]}
+    tasks[stages] = tasks.get(stages, []) + [halo_values]
+    tasks[stages + 1] = tasks.get(stages + 1, []) + [short_sum]
+    for step in range(1, 2 * stages):
+        if step == 2:
+            start_all(halo[0::2])
+        for task in tasks.get(step, []):
+            task()
+        order = range(colors - 1, -1, -1) if step == 1 else range(colors)
+        for k in order:
+            exchange(k, step)
+            if step == 2 * stages - 1:
+                inverse(k)
 
     out_ref[...] = (
         (masked_ref[...].astype(F32) + gcol_ref[:, 6:7] * total_ref[...])
@@ -379,15 +410,17 @@
     basis = radial_weight.shape[0]
     waves = wavevectors.shape[1]
     n = lax.axis_size("space")
-    stages = n.bit_length() - 1
-    assert n == 1 << stages and cells == GRID * GRID
+    power = n.bit_length() - 1
+    assert n == 1 << power and power >= 3 and cells == GRID * GRID
+    widths = (2,) + (2,) * ((power - 1) % 2) + (4,) * ((power - 1) // 2)
+    stages = len(widths)
     atoms = cells * slots
     rows = 2 * feats // n
     colors = len(PLANS)
     lanes = waves // colors
     dims = (
         n,
-        stages,
+        widths,
         cells,
         slots,
         feats,
@@ -429,8 +462,8 @@
             pltpu.SemaphoreType.DMA((6,)),
             pltpu.SemaphoreType.DMA((2, 2)),
             pltpu.SemaphoreType.DMA((2, 2)),
-            pltpu.SemaphoreType.DMA((colors, 2 * stages)),
-            pltpu.SemaphoreType.DMA((colors, 2 * stages)),
+            pltpu.SemaphoreType.DMA((colors, 2 * stages, max(widths) - 1)),
+            pltpu.SemaphoreType.DMA((colors, 2 * stages, max(widths) - 1)),
         ],
         compiler_params=pltpu.CompilerParams(collective_id=0, has_side_effects=True),
         name="ewald_layer",

time: 46.6 us -> 35.7 us (0.77)
  Pallas kernels: 44.8 us -> 33.9 us
    pallas_call x1, Pallas kernels: 44.8 us -> 33.9 us  [local(): pl.pallas_call(functools.partial(layer_kernel, dims), out_shape=jax.Shape...]
where the time goes in v3:
time: 35.7 us; the launch traced here: 35.5 us
  Pallas kernels  33.9 us (95%)
  local copies, waits for them, and re-layouts  1.58 us (4%)
    pallas_call x1, Pallas kernels, local(): pl.pallas_call(functools.partial(layer_kernel, dims), out_shape=jax.Shape...  33.9 us
    unnamed x1, local copies, waits for them, and re-layouts  1.58 us

profile of v3, /device:TPU:0, one launch (start us, length us, event | category | flops | bytes accessed | tf_op | source)
XLA Modules:
  0.0 35.5 jit_solution(16030558309534807297)
XLA Ops:
  0.0 33.9 %ewald_layer.1 = bf16[9,32,256]{2,1,0:T(8,128)(2,1)} custom-call(s32[9]{0:T(128)} %counts_ref.1, bf16[9,32,256]{2,1,0:T(8,128)(2,1)} %x_hbm.1, bf16[9,3,32]{2,1,0:T(4,128)(2,1)} %off_hbm.1, s32[3,1024]{1,0:T(4,128)} %wave_hbm.1, bf16[256,256]{1,0:T(8,128)(2,1)} %charge_hbm.1, f32[4,256]{1,0:T(4,128)} %filter_hbm.1, bf16[4,256,256]{2,1,0:T(8,128)(2,1)} %radial_hbm.1), custom_call_target="tpu_custom_call" | custom-call | tf_op jit(solution)/shard_map/ewald_layer/pallas_call | solution.py:434
  33.9 1.6 %copy.9 = bf16[9,32,256]{2,1,0:T(8,128)(2,1)} copy(bf16[9,32,256]{2,1,0:T(8,128)(2,1)} %ewald_layer.1) | data formatting | bytes 294912

commit v4 on v3

--- a/solution.py
+++ b/solution.py
@@ -166,7 +166,6 @@
     length = (2.0 * math.pi) * jnp.sqrt(tx * tx + ty * ty + tz * tz)
     wave_ref[...] = jnp.concatenate([tx, ty, tz, length, jnp.zeros((4, waves), F32)], axis=0)
 
-    pl.semaphore_wait(barrier, len(peers))
     halo = []
     for slot, peer in ((0, above), (1, below)):
         for which, src, dst in ((0, masked_ref, halo_x), (1, geo_ref, halo_geo)):
@@ -214,6 +213,25 @@
             for d in range(1, widths[digit])
         ]
 
+    def core_copy(k, d):
+        digit = orders[k][1]
+        part = size_of(k, 2)
+        where = (digits[digit] - d + widths[digit]) % widths[digit]
+        place = full_ref.at[k, pl.ds(lo_of(k, 1) + where * part, part)]
+        return pltpu.make_async_remote_copy(
+            src_ref=place,
+            dst_ref=place,
+            send_sem=send_sem.at[k, stages, d],
+            recv_sem=recv_sem.at[k, stages, d],
+            device_id={"space": partners[0][0]},
+            device_id_type=MESH,
+        )
+
+    def start_gather(k, s):
+        start_all(gather_copies(k, s))
+        if s == 1:
+            core_copy(k, 0).start()
+
     def start_all(copies):
         for copy in copies:
             copy.start()
@@ -252,7 +270,7 @@
                 offset_k = (magnitude - 3.0 * b) * (1.0 / 3.0)
                 gain = gain + weights[:, b : b + 1] * jnp.exp(-(offset_k * offset_k))
             full_ref[k, keep] = (summed * gain).astype(BF16)
-            start_all(gather_copies(k, s))
+            start_gather(k, s)
 
     def inverse(k):
         recip = jnp.zeros((atoms, feats), F32)
@@ -268,9 +286,16 @@
             scatter_finish(k, step)
         else:
             s = 2 * stages - 1 - step
-            wait_all(gather_copies(k, s))
-            if s:
-                start_all(gather_copies(k, s - 1))
+            if s == 0:
+                wait_all([core_copy(k, d) for d in range(widths[orders[k][1]])])
+            elif s == 1:
+                for d, copy in enumerate(gather_copies(k, 1)):
+                    copy.wait_recv()
+                    core_copy(k, d + 1).start()
+                    copy.wait_send()
+            else:
+                wait_all(gather_copies(k, s))
+                start_gather(k, s - 1)
 
     loads[3].wait()
     charges = jnp.dot(masked_ref[...], charge_ref[...], preferred_element_type=F32)
@@ -298,6 +323,9 @@
         acc_ref[k, 0 : n // 2] = real.reshape(n // 2, rows, lanes).astype(BF16)
         imag = jnp.dot(charges_t, sin_ref[k], preferred_element_type=F32)
         acc_ref[k, n // 2 : n] = imag.reshape(n // 2, rows, lanes).astype(BF16)
+        if k == 0:
+            pl.semaphore_wait(barrier, len(peers))
+            start_all(halo[1::2])
         start_all(scatter_copies(k, 0))
 
     def near_values(source, layer):
@@ -378,7 +406,6 @@
             short = short + jnp.dot(pair_ref[b], vals_ref[b], preferred_element_type=F32)
         total_ref[...] = short * scale_short
 
-    start_all(halo[1::2])
     for k in range(colors):
         tables(k, functools.partial(exchange, k - 1, 0) if k else lambda: None)
     exchange(colors - 1, 0)
@@ -462,8 +489,8 @@
             pltpu.SemaphoreType.DMA((6,)),
             pltpu.SemaphoreType.DMA((2, 2)),
             pltpu.SemaphoreType.DMA((2, 2)),
-            pltpu.SemaphoreType.DMA((colors, 2 * stages, max(widths) - 1)),
-            pltpu.SemaphoreType.DMA((colors, 2 * stages, max(widths) - 1)),
+            pltpu.SemaphoreType.DMA((colors, 2 * stages, max(widths))),
+            pltpu.SemaphoreType.DMA((colors, 2 * stages, max(widths))),
         ],
         compiler_params=pltpu.CompilerParams(collective_id=0, has_side_effects=True),
         name="ewald_layer",

time: 35.7 us -> 35.2 us (0.986)
  Pallas kernels: 33.9 us -> 33.4 us
    pallas_call x1, Pallas kernels: 33.9 us -> 33.4 us  [local(): pl.pallas_call(functools.partial(layer_kernel, dims), out_shape=jax.Shape...]
where the time goes in v4:
time: 35.2 us; the launch traced here: 35 us
  Pallas kernels  33.4 us (95%)
  local copies, waits for them, and re-layouts  1.58 us (4%)
    pallas_call x1, Pallas kernels, local(): pl.pallas_call(functools.partial(layer_kernel, dims), out_shape=jax.Shape...  33.4 us
    unnamed x1, local copies, waits for them, and re-layouts  1.58 us

profile of v4, /device:TPU:0, one launch (start us, length us, event | category | flops | bytes accessed | tf_op | source)
XLA Modules:
  0.0 35.0 jit_solution(943107836628621482)
XLA Ops:
  0.0 33.4 %ewald_layer.1 = bf16[9,32,256]{2,1,0:T(8,128)(2,1)} custom-call(s32[9]{0:T(128)} %counts_ref.1, bf16[9,32,256]{2,1,0:T(8,128)(2,1)} %x_hbm.1, bf16[9,3,32]{2,1,0:T(4,128)(2,1)} %off_hbm.1, s32[3,1024]{1,0:T(4,128)} %wave_hbm.1, bf16[256,256]{1,0:T(8,128)(2,1)} %charge_hbm.1, f32[4,256]{1,0:T(4,128)} %filter_hbm.1, bf16[4,256,256]{2,1,0:T(8,128)(2,1)} %radial_hbm.1), custom_call_target="tpu_custom_call" | custom-call | tf_op jit(solution)/shard_map/ewald_layer/pallas_call | solution.py:461
  33.4 1.6 %copy.9 = bf16[9,32,256]{2,1,0:T(8,128)(2,1)} copy(bf16[9,32,256]{2,1,0:T(8,128)(2,1)} %ewald_layer.1) | data formatting | bytes 294912

commit v5 on v4

--- a/solution.py
+++ b/solution.py
@@ -317,7 +317,7 @@
             sin_ref[k, at, :] = (u * poly(SIN_TURN, sq)).astype(BF16)
             return carry
 
-        lax.fori_loop(0, atoms // 32, table_rows, 0)
+        lax.fori_loop(0, atoms // 32, table_rows, 0, unroll=3)
         between()
         real = jnp.dot(charges_t, cos_ref[k], preferred_element_type=F32)
         acc_ref[k, 0 : n // 2] = real.reshape(n // 2, rows, lanes).astype(BF16)
@@ -419,7 +419,7 @@
             start_all(halo[0::2])
         for task in tasks.get(step, []):
             task()
-        order = range(colors - 1, -1, -1) if step == 1 else range(colors)
+        order = range(colors - 1, -1, -1) if step in (1, 2 * stages - 2, 2 * stages - 1) else range(colors)
         for k in order:
             exchange(k, step)
             if step == 2 * stages - 1:

time: 35.2 us -> 34.8 us (0.989)
  Pallas kernels: 33.4 us -> 32.9 us
    pallas_call x1, Pallas kernels: 33.4 us -> 32.9 us  [local(): pl.pallas_call(functools.partial(layer_kernel, dims), out_shape=jax.Shape...]
where the time goes in v5:
time: 34.8 us; the launch traced here: 34.5 us
  Pallas kernels  32.9 us (95%)
  local copies, waits for them, and re-layouts  1.58 us (5%)
    pallas_call x1, Pallas kernels, local(): pl.pallas_call(functools.partial(layer_kernel, dims), out_shape=jax.Shape...  32.9 us
    unnamed x1, local copies, waits for them, and re-layouts  1.58 us

profile of v5, /device:TPU:0, one launch (start us, length us, event | category | flops | bytes accessed | tf_op | source)
XLA Modules:
  0.0 34.5 jit_solution(501623757652636885)
XLA Ops:
  0.0 32.9 %ewald_layer.1 = bf16[9,32,256]{2,1,0:T(8,128)(2,1)} custom-call(s32[9]{0:T(128)} %counts_ref.1, bf16[9,32,256]{2,1,0:T(8,128)(2,1)} %x_hbm.1, bf16[9,3,32]{2,1,0:T(4,128)(2,1)} %off_hbm.1, s32[3,1024]{1,0:T(4,128)} %wave_hbm.1, bf16[256,256]{1,0:T(8,128)(2,1)} %charge_hbm.1, f32[4,256]{1,0:T(4,128)} %filter_hbm.1, bf16[4,256,256]{2,1,0:T(8,128)(2,1)} %radial_hbm.1), custom_call_target="tpu_custom_call" | custom-call | tf_op jit(solution)/shard_map/ewald_layer/pallas_call | solution.py:461
  32.9 1.6 %copy.9 = bf16[9,32,256]{2,1,0:T(8,128)(2,1)} copy(bf16[9,32,256]{2,1,0:T(8,128)(2,1)} %ewald_layer.1) | data formatting | bytes 294912
